TPU v7x, 256 devices: a whole 4x4x8 slice. The times are simulated.
256 devices in a mesh: sub: 8 (over z), row: 2 (over core), col: 16 (over y, x).
Axes of the slice: x: 4, y: 4, z: 8, core: 2. Of those that a mesh axis runs over, the one named last changes fastest.
Arguments:
- factor_cols: bfloat16 [8, 2, 2048, 4096], P('sub', None, 'col', 'row'), may hold values from -0.09375 to 0.09375
- block_pattern: int32 [8, 16, 16], P('sub'), may hold values 0 or 1
- diag_inverse: float32 [8, 4096, 2048], P('sub', ('row', 'col')), may hold values from -1 to 2
- coupling_cols: bfloat16 [8, 2, 2048, 1024], P('sub', 'row', 'col'), may hold values from -0.09375 to 0.09375
- separator_rows: int32 [8, 1024], P('sub'), may hold values from 0 to 1535, as said below
- root_inverse: float32 [1536, 1536], P('col'), may hold values from -1 to 2
- right_side: float32 [8, 4096, 128], P('sub', 'row'), may hold values from -6 to 6
- root_right: float32 [1536, 128], P('col'), may hold values from -6 to 6
Outputs:
- solution: float32 [8, 4096, 128], P('sub', ('row', 'col'))
- root_solution: float32 [1536, 128], P('col')
Inputs may be any that keep to these rules, and one draw needn't show every extreme that they name: `separator_rows`: within one section the 1024 entries are distinct.
All inputs are finite; a program needn't handle non-finite values. No bound on the sum of `block_pattern` on one device may be relied on, other than what follows from the above.
Results may differ from a plain program's by a relative error of at most 0.003.
Values may be sent and summed in bfloat16 or wider, within the bound.
No kernel may reach another device: no remote copies, remote signals or barrier semaphores. Data moves between devices by JAX's collectives and lax.ppermute only.
A program may use at most 64 MiB of HBM per device.

v0:
```python
import jax
import jax.numpy as jnp
from jax import lax
from jax.sharding import PartitionSpec as P

BLOCK = 256
SEPARATOR = 1536
precise = lax.Precision.HIGHEST
first_axes = (((0,), (0,)), ((), ()))


def spread(block, axis, source):
    block = jnp.where(lax.axis_index(axis) == source, block, jnp.zeros_like(block))
    return lax.psum(block, axis)


def shards(
    factor_cols,
    block_pattern,
    diag_inverse,
    coupling_cols,
    separator_rows,
    root_inverse,
    right_side,
    root_right,
):
    factor = factor_cols[0]
    table = block_pattern[0]
    inverse = diag_inverse[0]
    couple_own = coupling_cols[0, 0]
    right_rows = right_side[0]
    rows_sep = separator_rows[0]
    panel_count, col_width, panel_rows = factor.shape
    sources = right_rows.shape[1]
    block_count = table.shape[1]
    row_id = lax.axis_index("row")
    col_id = lax.axis_index("col")
    sub_id = lax.axis_index("sub")
    own_blocks = lax.dynamic_slice_in_dim(
        table, row_id * (panel_rows // BLOCK), panel_rows // BLOCK, 0
    ).astype(jnp.float32)
    row_mask = jnp.repeat(own_blocks, BLOCK, axis=0)
    col_pos = (
        jnp.arange(panel_count)[:, None] * panel_rows
        + col_id * col_width
        + jnp.arange(col_width)[None, :]
    )
    selector = (jnp.arange(block_count)[:, None, None] == (col_pos // BLOCK)[None]).astype(
        jnp.float32
    )
    pattern_mask = jnp.einsum("in,nqj->qji", row_mask, selector)
    below_mask = (jnp.arange(panel_count) < row_id).astype(jnp.float32)[:, None, None]
    masked = factor * (pattern_mask * below_mask).astype(jnp.bfloat16)
    zero_panel = jnp.zeros((panel_rows, sources), jnp.float32)
    zero_share = jnp.zeros((col_width, sources), jnp.float32)

    def forward(current, carried):
        accumulated, solved = carried
        panel_total = lax.psum(accumulated, "col")
        solved = lax.cond(
            row_id == current,
            lambda values: jnp.dot(
                inverse, right_rows - values, precision=precise, preferred_element_type=jnp.float32
            ),
            lambda values: solved,
            panel_total,
        )
        received = spread(solved.astype(jnp.bfloat16), "row", current)
        factor_now = lax.dynamic_index_in_dim(masked, current, 0, keepdims=False)
        accumulated = accumulated + lax.dot_general(
            factor_now, received, first_axes, preferred_element_type=jnp.float32
        )
        return (accumulated, solved)

    accumulated, solved = lax.fori_loop(0, panel_count, forward, (zero_panel, zero_share))
    own_low = solved.astype(jnp.bfloat16)
    sep_partial = lax.dot_general(
        couple_own, own_low, first_axes, preferred_element_type=jnp.float32
    )
    onehot = (jnp.arange(SEPARATOR)[:, None] == rows_sep[None, :]).astype(jnp.float32)
    mapped = jnp.dot(onehot, sep_partial, precision=precise, preferred_element_type=jnp.float32)
    share_rows = root_inverse.shape[0]
    slice_start = col_id * share_rows
    first_device = ((sub_id == 0) & (row_id == 0)).astype(jnp.float32)
    own_rows = (
        lax.dynamic_slice_in_dim(-mapped, slice_start, share_rows, 0) + first_device * root_right
    )
    root_term = lax.dynamic_update_slice_in_dim(-mapped, own_rows, slice_start, 0)
    root_rhs = lax.psum(root_term, ("sub", "row", "col"))
    root_half = jnp.dot(
        root_inverse, root_rhs, precision=precise, preferred_element_type=jnp.float32
    )
    root_part = lax.psum_scatter(
        lax.dot_general(
            root_inverse,
            root_half,
            first_axes,
            precision=precise,
            preferred_element_type=jnp.float32,
        ),
        "col",
        scatter_dimension=0,
        tiled=True,
    )
    root_full = lax.all_gather(root_part.astype(jnp.bfloat16), "col", axis=0, tiled=True).astype(
        root_part.dtype
    )
    picked = lax.dot_general(
        onehot, root_full, first_axes, precision=precise, preferred_element_type=jnp.float32
    ).astype(jnp.bfloat16)
    couple_back = jnp.dot(couple_own, picked, preferred_element_type=jnp.float32)

    def backward(counter, carried):
        finished, panel_low = carried
        current = panel_count - 1 - counter
        factor_now = lax.dynamic_index_in_dim(masked, current, 0, keepdims=False)
        contribution = jnp.dot(factor_now, panel_low, preferred_element_type=jnp.float32)
        own_couple = couple_back * (row_id == current).astype(jnp.float32)
        summed = lax.psum(contribution + own_couple, "row")
        partial_value = lax.cond(
            row_id == current,
            lambda values: lax.dot_general(
                inverse,
                solved - values,
                first_axes,
                precision=precise,
                preferred_element_type=jnp.float32,
            ),
            lambda values: zero_panel,
            summed,
        )
        value = lax.psum_scatter(partial_value, "col", scatter_dimension=0, tiled=True)
        whole_low = lax.all_gather(value.astype(jnp.bfloat16), "col", axis=0, tiled=True)
        active = row_id == current
        finished = jnp.where(active, value, finished)
        panel_low = jnp.where(active, whole_low, panel_low)
        return (finished, panel_low)

    finished, panel_low = lax.fori_loop(
        0, panel_count, backward, (zero_share, zero_panel.astype(jnp.bfloat16))
    )
    return (finished[None], root_part)


def solution(mesh):
    return jax.shard_map(
        shards,
        mesh=mesh,
        in_specs=(
            P("sub", None, "col", "row"),
            P("sub", None, None),
            P("sub", ("row", "col"), None),
            P("sub", "row", "col", None),
            P("sub", None),
            P("col", None),
            P("sub", "row", None),
            P("col", None),
        ),
        out_specs=(P("sub", ("row", "col"), None), P("col", None)),
        check_vma=False,
    )
```

profile of v0, /device:TPU:32, one launch (start us, length us, event | category | flops | bytes accessed | tf_op | source)
XLA Modules:
  0.0 886.8 jit_solution(2642969435639359948)
XLA Ops:
  8.0 0.7 convert_bitcast_fusion
  8.8 0.1 copy.21
  8.9 0.1 broadcast_in_dim.25
  9.0 0.1 and_select_fusion
  9.1 2.8 fusion.15
  11.9 221.9 %while.37 = (s32[]{:T(128)}, f32[2048,128]{1,0:T(8,128)}, f32[128,128]{0,1:T(8,128)S(1)}, bf16[2,128,2048]{2,1,0:T(8,128)(2,1)}, s32[]{:T(128)}, /*index=5*/f32[...) while((s32[]{:T(128)}, f32[2048,128]{1,0:T(8,128)}, ...), condition=%wide.region_5.6_spmd.clone, body=%wide.region_0.5_spmd.clone.sunk | while | flops 470859776 | bytes 18612512 | solution.py:75
  11.9 0.0 all-reduce.6.cloned.1.call-start
  12.0 1.1 broadcast_select_fusion.7
  13.1 0.0 all-reduce.6.cloned.1.call-update
  13.1 103.1 %all-reduce.6.cloned.1.call-done = f32[2048,128]{1,0:T(8,128)} async-done(((f32[2048,128]{1,0:T(8,128)}), f32[2048,128]{1,0:T(8,128)}) %all-reduce.6.cloned.1.call-update) | async-done | bytes 1048592 | tf_op jit(solution)/shard_map/while/body/eval_jaxpr/psum | solution.py:59
  116.2 3.5 conditional.7
  116.2 3.5 convolution_bitcast_fusion.1
  119.7 3.4 psum.51
  123.1 2.4 convolution_add_fusion.4
  125.5 2.3 broadcast_select_fusion.7
  127.8 0.0 all-reduce.6.cloned.1.call-update
  127.8 98.6 %all-reduce.6.cloned.1.call-done = f32[2048,128]{1,0:T(8,128)} async-done(((f32[2048,128]{1,0:T(8,128)}), f32[2048,128]{1,0:T(8,128)}) %all-reduce.6.cloned.1.call-update) | async-done | bytes 1048592 | tf_op jit(solution)/shard_map/while/body/eval_jaxpr/psum | solution.py:59
  226.4 5.1 psum.51
  231.4 2.4 convolution_add_fusion.4
  233.8 0.2 fusion.19
  234.0 2.9 fusion.16
  237.0 0.9 copy-done.5
  237.9 0.0 all-reduce.4.cloned.1.call-update
  237.9 0.0 reduce-scatter.5.cloned.1.call-start
  238.0 252.3 %all-reduce.4.cloned.1.call-done = f32[1536,128]{1,0:T(8,128)} async-done(((f32[1536,128]{1,0:T(8,128)}), f32[1536,128]{1,0:T(8,128)}) %all-reduce.4.cloned.1.call-update) | async-done | bytes 786448 | tf_op jit(solution)/shard_map/psum | solution.py:89
  490.3 1.9 fusion.24
  492.2 0.8 convolution_bitcast_fusion.2
  493.0 1.2 copy.27
  494.2 0.0 reduce-scatter.5.cloned.1.call-update
  494.2 0.1 copy.24
  494.3 79.0 %reduce-scatter.5.cloned.1.call-done = f32[96,128]{1,0:T(8,128)} async-done(((f32[1536,128]{1,0:T(8,128)}), f32[96,128]{1,0:T(8,128)}) %reduce-scatter.5.cloned.1.call-update) | async-done | bytes 49168 | tf_op jit(solution)/shard_map/reduce_scatter | solution.py:93
  573.4 0.8 convert_element_type.87
  574.2 23.4 %all_gather.13 = bf16[1536,128]{1,0:T(8,128)(2,1)S(1)} all-gather(bf16[96,128]{1,0:T(8,128)(2,1)S(1)} %convert_element_type.87), channel_id=1, replica_groups=mesh['sub'=8,'row'=2,'col'=16] {'col'}, dimensions={0}, use_global_device_ids=true | all-gather | bytes 417792 | tf_op jit(solution)/shard_map/all_gather | solution.py:105
  597.6 1.8 fusion.17
  599.4 0.3 convolution_bitcast_fusion.3
  599.6 0.1 copy.23
  599.7 278.9 %while.38 = (s32[]{:T(128)}, f32[128,128]{0,1:T(8,128)S(1)}, bf16[2048,128]{0,1:T(8,128)(2,1)S(1)}, s32[]{:T(128)}, bf16[2,128,2048]{2,1,0:T(8,128)(2,1)}, /*ind...) while((s32[]{:T(128)}, f32[128,128]{0,1:T(8,128)S(1)}, ...), condition=%wide.region_13.14_spmd.clone, body=%wide.region_8.13_spmd.clone.sunk | while | flops 470663168 | bytes 13697360 | solution.py:139
  599.8 0.0 all-reduce.8.cloned.1.call-start
  599.8 2.0 convolution_add_fusion.5
  601.8 0.0 all-reduce.8.cloned.1.call-update
  601.8 0.0 reduce-scatter.7.cloned.1.call-start
  601.9 29.3 %all-reduce.8.cloned.1.call-done = f32[128,128]{1,0:T(8,128)} async-done(((f32[128,128]{1,0:T(8,128)}), f32[128,128]{1,0:T(8,128)}) %all-reduce.8.cloned.1.call-update) | async-done | bytes 65552 | tf_op jit(solution)/shard_map/while/body/eval_jaxpr/psum | solution.py:119
  631.2 0.1 conditional.8
  631.2 0.1 broadcast_in_dim.1
  631.3 1.0 copy-done.3
  632.3 0.0 reduce-scatter.7.cloned.1.call-update
  632.3 81.8 %reduce-scatter.7.cloned.1.call-done = f32[128,128]{0,1:T(8,128)} async-done(((f32[2048,128]{0,1:T(8,128)}), f32[128,128]{0,1:T(8,128)}) %reduce-scatter.7.cloned.1.call-update) | async-done | bytes 65552 | tf_op jit(solution)/shard_map/while/body/eval_jaxpr/reduce_scatter | solution.py:132
  714.2 0.9 fusion.43
  715.1 24.0 %all_gather.16 = bf16[2048,128]{0,1:T(8,128)(2,1)S(1)} all-gather(bf16[128,128]{0,1:T(8,128)(2,1)S(1)} %get-tuple-element.583), channel_id=1, replica_groups=mesh['sub'=8,'row'=2,'col'=16] {'col'}, dimensions={0}, use_global_device_ids=true | all-gather | bytes 557056 | tf_op jit(solution)/shard_map/while/body/eval_jaxpr/all_gather | solution.py:133
  739.1 0.2 broadcast_select_fusion.9
  739.4 0.0 all-reduce.8.cloned.1.call-start
  739.4 2.0 convolution_add_fusion.5
  741.4 0.0 all-reduce.8.cloned.1.call-update
  741.4 0.0 reduce-scatter.7.cloned.1.call-start
  741.5 29.0 %all-reduce.8.cloned.1.call-done = f32[128,128]{1,0:T(8,128)} async-done(((f32[128,128]{1,0:T(8,128)}), f32[128,128]{1,0:T(8,128)}) %all-reduce.8.cloned.1.call-update) | async-done | bytes 65552 | tf_op jit(solution)/shard_map/while/body/eval_jaxpr/psum | solution.py:119
  770.5 1.9 conditional.8
  770.5 1.9 convolution_bitcast_fusion
  772.4 1.0 copy-done.3
  773.4 0.0 reduce-scatter.7.cloned.1.call-update
  773.4 80.0 %reduce-scatter.7.cloned.1.call-done = f32[128,128]{0,1:T(8,128)} async-done(((f32[2048,128]{0,1:T(8,128)}), f32[128,128]{0,1:T(8,128)}) %reduce-scatter.7.cloned.1.call-update) | async-done | bytes 65552 | tf_op jit(solution)/shard_map/while/body/eval_jaxpr/reduce_scatter | solution.py:132
  853.5 0.9 fusion.43
  854.4 24.0 %all_gather.16 = bf16[2048,128]{0,1:T(8,128)(2,1)S(1)} all-gather(bf16[128,128]{0,1:T(8,128)(2,1)S(1)} %get-tuple-element.583), channel_id=1, replica_groups=mesh['sub'=8,'row'=2,'col'=16] {'col'}, dimensions={0}, use_global_device_ids=true | all-gather | bytes 557056 | tf_op jit(solution)/shard_map/while/body/eval_jaxpr/all_gather | solution.py:133
  878.4 0.2 broadcast_select_fusion.9
  878.6 0.7 copy.25
  (30 shorter events, 0.1 us)
Async XLA Ops:
  8.0 482.3 %copy-start = (f32[96,1536]{1,0:T(8,128)S(1)}, f32[96,1536]{1,0:T(8,128)}, u32[]{:S(2)}) copy-start(f32[96,1536]{1,0:T(8,128)} %param.21) | copy-start | bytes 1769476
  9.1 2.8 copy-start.2
  11.9 221.9 %copy-start.4 = (bf16[1,1,128,1024]{3,2,1,0:T(8,128)(2,1)S(1)}, bf16[1,1,128,1024]{3,2,1,0:T(8,128)(2,1)}, u32[]{:S(2)}) copy-start(bf16[1,1,128,1024]{3,2,1,0:T(8,128)(2,1)} %param.19) | copy-start | bytes 786436
  11.9 222.1 %copy-start.7 = (s32[1,1024]{1,0:T(1,128)S(1)}, s32[1,1024]{1,0:T(1,128)}, u32[]{:S(2)}) copy-start(s32[1,1024]{1,0:T(1,128)} %param.20) | copy-start | bytes 12292
  11.9 104.2 %all-reduce.6.cloned.1.call-start = ((), (), s32[]{:S(2)}) async-start(), calls=%async_computation.4 | async-start | bytes 2097152 | tf_op jit(solution)/shard_map/while/body/eval_jaxpr/psum | solution.py:59
  116.2 6.9 copy-start.1
  125.5 100.9 %all-reduce.6.cloned.1.call-start = ((), (), s32[]{:S(2)}) async-start(), calls=%async_computation.4 | async-start | bytes 2097152 | tf_op jit(solution)/shard_map/while/body/eval_jaxpr/psum | solution.py:59
  226.4 5.1 copy-start.1
  233.8 256.5 %all-reduce.4.cloned.1.call-start = ((), (), s32[]{:S(2)}) async-start(), calls=%async_computation.2 | async-start | bytes 1572864 | tf_op jit(solution)/shard_map/psum | solution.py:89
  234.0 2.9 copy-start.6
  237.0 0.9 copy-start.5
  237.9 335.5 %reduce-scatter.5.cloned.1.call-start = ((), (), s32[]{:S(2)}) async-start(), calls=%async_computation.3 | async-start | bytes 835584 | tf_op jit(solution)/shard_map/reduce_scatter | solution.py:93
  599.8 31.4 %all-reduce.8.cloned.1.call-start = ((), (), s32[]{:S(2)}) async-start(), calls=%async_computation.5 | async-start | bytes 131072 | tf_op jit(solution)/shard_map/while/body/eval_jaxpr/psum | solution.py:119
  601.8 112.3 %reduce-scatter.7.cloned.1.call-start = ((), (), s32[]{:S(2)}) async-start(), calls=%async_computation.6 | async-start | bytes 1114112 | tf_op jit(solution)/shard_map/while/body/eval_jaxpr/reduce_scatter | solution.py:132
  631.3 1.0 copy-start.3
  739.4 31.1 %all-reduce.8.cloned.1.call-start = ((), (), s32[]{:S(2)}) async-start(), calls=%async_computation.5 | async-start | bytes 131072 | tf_op jit(solution)/shard_map/while/body/eval_jaxpr/psum | solution.py:119
  741.4 112.0 %reduce-scatter.7.cloned.1.call-start = ((), (), s32[]{:S(2)}) async-start(), calls=%async_computation.6 | async-start | bytes 1114112 | tf_op jit(solution)/shard_map/while/body/eval_jaxpr/reduce_scatter | solution.py:132
  772.4 1.0 copy-start.3
Sparse Core Ops, SparseCore 0:
  16.4 99.7 all-reduce.5
  129.9 96.4 all-reduce.5
  603.9 27.2 all-reduce.7
  635.0 79.1 reduce-scatter.6
  743.2 27.2 all-reduce.7
  774.3 79.1 reduce-scatter.6
Sparse Core Ops, SparseCore 1:
  239.7 250.5 all-reduce.3
  494.6 78.7 reduce-scatter.4
where the time goes:
time: 888 us; the launch traced here: 887 us
  waiting for transfers between devices  753 us (85%)
  blocking collectives  79.9 us (9%)
  matrix products  24.7 us (3%)
  between operations  15.7 us (2%)
    psum x1, waiting for transfers between devices, shards(): root_rhs = lax.psum(root_term, ('sub', 'row', 'col'))  252 us
    psum x2, waiting for transfers between devices, forward(): panel_total = lax.psum(accumulated, 'col')  202 us
    reduce_scatter x2, waiting for transfers between devices, backward(): lax.psum_scatter(partial_value, 'col', scatter_dimension=0, tiled=True)  162 us
    reduce_scatter x1, waiting for transfers between devices, shards(): lax.psum_scatter(lax.dot_general(root_inverse, root_half, first_axes, pre...  79 us
    psum x2, waiting for transfers between devices, backward(): summed = lax.psum(contribution + own_couple, 'row')  58.3 us
    all_gather x2, blocking collectives, backward(): lax.all_gather(value.astype(jnp.bfloat16), 'col', axis=0, tiled=True)  48.1 us
    all_gather x1, blocking collectives, shards(): lax.all_gather(root_part.astype(jnp.bfloat16), 'col', axis=0, tiled=True)  23.4 us
  transfers between devices with their start and end apart: 8, of which 8 were waited for; matrix products, arithmetic and copies ran while one was open for 0% of the time, Pallas kernels for 0%

commit v1 on v0

--- a/solution.py
+++ b/solution.py
@@ -86,7 +86,7 @@
         lax.dynamic_slice_in_dim(-mapped, slice_start, share_rows, 0) + first_device * root_right
     )
     root_term = lax.dynamic_update_slice_in_dim(-mapped, own_rows, slice_start, 0)
-    root_rhs = lax.psum(root_term, ("sub", "row", "col"))
+    root_rhs = lax.psum(lax.psum(root_term, "sub"), ("row", "col"))
     root_half = jnp.dot(
         root_inverse, root_rhs, precision=precise, preferred_element_type=jnp.float32
     )

time: 888 us -> 823 us (0.927)
  waiting for transfers between devices: 753 us -> 689 us
    psum x1 -> x2, waiting for transfers between devices: 252 us -> 189 us  [shards(): root_rhs = lax.psum(lax.psum(root_term, 'sub'), ('row', 'col'))]
  transfers between devices with their start and end apart: 8 -> 9, of which waited for: 8 -> 9; matrix products, arithmetic and copies ran while one was open for 0% -> 0% of each run, Pallas kernels for 0% -> 0%
where the time goes in v1:
time: 823 us; the launch traced here: 822 us
  waiting for transfers between devices  689 us (84%)
  blocking collectives  79.9 us (10%)
  matrix products  24.7 us (3%)
  between operations  15.8 us (2%)
    psum x2, waiting for transfers between devices, forward(): panel_total = lax.psum(accumulated, 'col')  202 us
    psum x2, waiting for transfers between devices, shards(): root_rhs = lax.psum(lax.psum(root_term, 'sub'), ('row', 'col'))  189 us
    reduce_scatter x2, waiting for transfers between devices, backward(): lax.psum_scatter(partial_value, 'col', scatter_dimension=0, tiled=True)  162 us
    reduce_scatter x1, waiting for transfers between devices, shards(): lax.psum_scatter(lax.dot_general(root_inverse, root_half, first_axes, pre...  77.9 us
    psum x2, waiting for transfers between devices, backward(): summed = lax.psum(contribution + own_couple, 'row')  58.3 us
    all_gather x2, blocking collectives, backward(): lax.all_gather(value.astype(jnp.bfloat16), 'col', axis=0, tiled=True)  48.1 us
    all_gather x1, blocking collectives, shards(): lax.all_gather(root_part.astype(jnp.bfloat16), 'col', axis=0, tiled=True)  23.4 us
  transfers between devices with their start and end apart: 9, of which 9 were waited for; matrix products, arithmetic and copies ran while one was open for 0% of the time, Pallas kernels for 0%

profile of v1, /device:TPU:32, one launch (start us, length us, event | category | flops | bytes accessed | tf_op | source)
XLA Modules:
  0.0 822.5 jit_solution(1459054851037543681)
XLA Ops:
  8.0 0.7 convert_bitcast_fusion
  8.8 0.1 copy.21
  8.9 0.1 broadcast_in_dim.25
  9.0 0.1 and_select_fusion
  9.1 2.8 fusion.15
  11.9 221.9 %while.37 = (s32[]{:T(128)}, f32[2048,128]{1,0:T(8,128)}, f32[128,128]{0,1:T(8,128)S(1)}, bf16[2,128,2048]{2,1,0:T(8,128)(2,1)}, s32[]{:T(128)}, /*index=5*/f32[...) while((s32[]{:T(128)}, f32[2048,128]{1,0:T(8,128)}, ...), condition=%wide.region_5.6_spmd.clone, body=%wide.region_0.5_spmd.clone.sunk | while | flops 470859776 | bytes 18612512 | solution.py:75
  11.9 0.0 all-reduce.9.cloned.1.call-start
  12.0 1.1 broadcast_select_fusion.7
  13.1 103.1 %all-reduce.9.cloned.1.call-done = f32[2048,128]{1,0:T(8,128)} async-done(((f32[2048,128]{1,0:T(8,128)}), f32[2048,128]{1,0:T(8,128)}) %all-reduce.9.cloned.1.call-update) | async-done | bytes 1048592 | tf_op jit(solution)/shard_map/while/body/eval_jaxpr/psum | solution.py:59
  116.2 3.5 conditional.7
  116.2 3.5 convolution_bitcast_fusion.1
  119.7 3.4 psum.59
  123.1 2.4 convolution_add_fusion.4
  125.5 2.3 broadcast_select_fusion.7
  127.8 98.5 %all-reduce.9.cloned.1.call-done = f32[2048,128]{1,0:T(8,128)} async-done(((f32[2048,128]{1,0:T(8,128)}), f32[2048,128]{1,0:T(8,128)}) %all-reduce.9.cloned.1.call-update) | async-done | bytes 1048592 | tf_op jit(solution)/shard_map/while/body/eval_jaxpr/psum | solution.py:59
  226.3 5.1 psum.59
  231.4 2.4 convolution_add_fusion.4
  233.8 0.2 fusion.19
  234.0 2.9 fusion.16
  237.0 0.9 copy-done.5
  237.9 0.0 all-reduce.5.cloned.1.call-update
  237.9 0.0 all-reduce.7.cloned.1.call-start
  238.0 73.4 %all-reduce.5.cloned.1.call-done = f32[1536,128]{1,0:T(8,128)} async-done(((f32[1536,128]{1,0:T(8,128)}), f32[1536,128]{1,0:T(8,128)}) %all-reduce.5.cloned.1.call-update) | async-done | bytes 786448 | tf_op jit(solution)/shard_map/psum | solution.py:89
  311.4 0.0 all-reduce.7.cloned.1.call-update
  311.4 0.0 reduce-scatter.5.cloned.1.call-start
  311.5 115.4 %all-reduce.7.cloned.1.call-done = f32[1536,128]{1,0:T(8,128)} async-done(((f32[1536,128]{1,0:T(8,128)}), f32[1536,128]{1,0:T(8,128)}) %all-reduce.7.cloned.1.call-update) | async-done | bytes 786448 | tf_op jit(solution)/shard_map/psum | solution.py:89
  426.9 1.9 fusion.24
  428.8 0.8 convolution_bitcast_fusion.2
  429.6 1.2 copy.27
  430.8 0.0 reduce-scatter.5.cloned.1.call-update
  430.9 0.1 copy.24
  431.0 77.9 %reduce-scatter.5.cloned.1.call-done = f32[96,128]{1,0:T(8,128)} async-done(((f32[1536,128]{1,0:T(8,128)}), f32[96,128]{1,0:T(8,128)}) %reduce-scatter.5.cloned.1.call-update) | async-done | bytes 49168 | tf_op jit(solution)/shard_map/reduce_scatter | solution.py:93
  508.9 0.8 convert_element_type.87
  509.7 23.4 %all_gather.13 = bf16[1536,128]{1,0:T(8,128)(2,1)S(1)} all-gather(bf16[96,128]{1,0:T(8,128)(2,1)S(1)} %convert_element_type.87), channel_id=1, replica_groups=mesh['sub'=8,'row'=2,'col'=16] {'col'}, dimensions={0}, use_global_device_ids=true | all-gather | bytes 417792 | tf_op jit(solution)/shard_map/all_gather | solution.py:105
  533.1 1.8 fusion.17
  534.9 0.3 convolution_bitcast_fusion.3
  535.1 0.1 copy.23
  535.2 278.9 %while.38 = (s32[]{:T(128)}, f32[128,128]{0,1:T(8,128)S(1)}, bf16[2048,128]{0,1:T(8,128)(2,1)S(1)}, s32[]{:T(128)}, bf16[2,128,2048]{2,1,0:T(8,128)(2,1)}, /*ind...) while((s32[]{:T(128)}, f32[128,128]{0,1:T(8,128)S(1)}, ...), condition=%wide.region_14.15_spmd.clone, body=%wide.region_9.14_spmd.clone.sunk | while | flops 470663168 | bytes 13697360 | solution.py:139
  535.2 0.0 all-reduce.11.cloned.1.call-start
  535.3 2.0 convolution_add_fusion.5
  537.3 0.0 all-reduce.11.cloned.1.call-update
  537.3 0.0 reduce-scatter.7.cloned.1.call-start
  537.4 29.3 %all-reduce.11.cloned.1.call-done = f32[128,128]{1,0:T(8,128)} async-done(((f32[128,128]{1,0:T(8,128)}), f32[128,128]{1,0:T(8,128)}) %all-reduce.11.cloned.1.call-update) | async-done | bytes 65552 | tf_op jit(solution)/shard_map/while/body/eval_jaxpr/psum | solution.py:119
  566.7 0.1 conditional.8
  566.7 0.1 broadcast_in_dim.1
  566.8 1.0 copy-done.3
  567.8 0.0 reduce-scatter.7.cloned.1.call-update
  567.8 81.8 %reduce-scatter.7.cloned.1.call-done = f32[128,128]{0,1:T(8,128)} async-done(((f32[2048,128]{0,1:T(8,128)}), f32[128,128]{0,1:T(8,128)}) %reduce-scatter.7.cloned.1.call-update) | async-done | bytes 65552 | tf_op jit(solution)/shard_map/while/body/eval_jaxpr/reduce_scatter | solution.py:132
  649.7 0.9 fusion.43
  650.6 24.0 %all_gather.16 = bf16[2048,128]{0,1:T(8,128)(2,1)S(1)} all-gather(bf16[128,128]{0,1:T(8,128)(2,1)S(1)} %get-tuple-element.583), channel_id=1, replica_groups=mesh['sub'=8,'row'=2,'col'=16] {'col'}, dimensions={0}, use_global_device_ids=true | all-gather | bytes 557056 | tf_op jit(solution)/shard_map/while/body/eval_jaxpr/all_gather | solution.py:133
  674.6 0.2 broadcast_select_fusion.9
  674.9 0.0 all-reduce.11.cloned.1.call-start
  674.9 2.0 convolution_add_fusion.5
  676.9 0.0 all-reduce.11.cloned.1.call-update
  676.9 0.0 reduce-scatter.7.cloned.1.call-start
  677.0 29.0 %all-reduce.11.cloned.1.call-done = f32[128,128]{1,0:T(8,128)} async-done(((f32[128,128]{1,0:T(8,128)}), f32[128,128]{1,0:T(8,128)}) %all-reduce.11.cloned.1.call-update) | async-done | bytes 65552 | tf_op jit(solution)/shard_map/while/body/eval_jaxpr/psum | solution.py:119
  706.0 1.9 conditional.8
  706.0 1.9 convolution_bitcast_fusion
  707.9 1.0 copy-done.3
  708.9 80.0 %reduce-scatter.7.cloned.1.call-done = f32[128,128]{0,1:T(8,128)} async-done(((f32[2048,128]{0,1:T(8,128)}), f32[128,128]{0,1:T(8,128)}) %reduce-scatter.7.cloned.1.call-update) | async-done | bytes 65552 | tf_op jit(solution)/shard_map/while/body/eval_jaxpr/reduce_scatter | solution.py:132
  789.0 0.9 fusion.43
  789.9 24.0 %all_gather.16 = bf16[2048,128]{0,1:T(8,128)(2,1)S(1)} all-gather(bf16[128,128]{0,1:T(8,128)(2,1)S(1)} %get-tuple-element.583), channel_id=1, replica_groups=mesh['sub'=8,'row'=2,'col'=16] {'col'}, dimensions={0}, use_global_device_ids=true | all-gather | bytes 557056 | tf_op jit(solution)/shard_map/while/body/eval_jaxpr/all_gather | solution.py:133
  813.9 0.2 broadcast_select_fusion.9
  814.1 0.7 copy.25
  (33 shorter events, 0.2 us)
Async XLA Ops:
  8.0 418.9 %copy-start = (f32[96,1536]{1,0:T(8,128)S(1)}, f32[96,1536]{1,0:T(8,128)}, u32[]{:S(2)}) copy-start(f32[96,1536]{1,0:T(8,128)} %param.21) | copy-start | bytes 1769476
  9.1 2.8 copy-start.2
  11.9 221.9 %copy-start.4 = (bf16[1,1,128,1024]{3,2,1,0:T(8,128)(2,1)S(1)}, bf16[1,1,128,1024]{3,2,1,0:T(8,128)(2,1)}, u32[]{:S(2)}) copy-start(bf16[1,1,128,1024]{3,2,1,0:T(8,128)(2,1)} %param.19) | copy-start | bytes 786436
  11.9 222.1 %copy-start.7 = (s32[1,1024]{1,0:T(1,128)S(1)}, s32[1,1024]{1,0:T(1,128)}, u32[]{:S(2)}) copy-start(s32[1,1024]{1,0:T(1,128)} %param.20) | copy-start | bytes 12292
  11.9 104.2 %all-reduce.9.cloned.1.call-start = ((), (), s32[]{:S(2)}) async-start(), calls=%async_computation.5 | async-start | bytes 2097152 | tf_op jit(solution)/shard_map/while/body/eval_jaxpr/psum | solution.py:59
  116.2 6.9 copy-start.1
  125.5 100.9 %all-reduce.9.cloned.1.call-start = ((), (), s32[]{:S(2)}) async-start(), calls=%async_computation.5 | async-start | bytes 2097152 | tf_op jit(solution)/shard_map/while/body/eval_jaxpr/psum | solution.py:59
  226.3 5.1 copy-start.1
  233.8 77.6 %all-reduce.5.cloned.1.call-start = ((), (), s32[]{:S(2)}) async-start(), calls=%async_computation.2 | async-start | bytes 1572864 | tf_op jit(solution)/shard_map/psum | solution.py:89
  234.0 2.9 copy-start.6
  237.0 0.9 copy-start.5
  237.9 189.0 %all-reduce.7.cloned.1.call-start = ((), (), s32[]{:S(2)}) async-start(), calls=%async_computation.3 | async-start | bytes 1572864 | tf_op jit(solution)/shard_map/psum | solution.py:89
  311.4 197.4 %reduce-scatter.5.cloned.1.call-start = ((), (), s32[]{:S(2)}) async-start(), calls=%async_computation.4 | async-start | bytes 835584 | tf_op jit(solution)/shard_map/reduce_scatter | solution.py:93
  535.2 31.5 %all-reduce.11.cloned.1.call-start = ((), (), s32[]{:S(2)}) async-start(), calls=%async_computation.6 | async-start | bytes 131072 | tf_op jit(solution)/shard_map/while/body/eval_jaxpr/psum | solution.py:119
  537.3 112.3 %reduce-scatter.7.cloned.1.call-start = ((), (), s32[]{:S(2)}) async-start(), calls=%async_computation.7 | async-start | bytes 1114112 | tf_op jit(solution)/shard_map/while/body/eval_jaxpr/reduce_scatter | solution.py:132
  566.8 1.0 copy-start.3
  674.9 31.1 %all-reduce.11.cloned.1.call-start = ((), (), s32[]{:S(2)}) async-start(), calls=%async_computation.6 | async-start | bytes 131072 | tf_op jit(solution)/shard_map/while/body/eval_jaxpr/psum | solution.py:119
  676.9 112.0 %reduce-scatter.7.cloned.1.call-start = ((), (), s32[]{:S(2)}) async-start(), calls=%async_computation.7 | async-start | bytes 1114112 | tf_op jit(solution)/shard_map/while/body/eval_jaxpr/reduce_scatter | solution.py:132
  707.9 1.0 copy-start.3
Sparse Core Ops, SparseCore 0:
  16.4 99.7 all-reduce.8
  129.9 96.4 all-reduce.8
  539.4 27.2 all-reduce.10
  570.5 79.1 reduce-scatter.6
  678.7 27.2 all-reduce.10
  709.8 79.1 reduce-scatter.6
Sparse Core Ops, SparseCore 1:
  238.0 73.3 all-reduce.4
  314.8 112.0 all-reduce.6
  431.2 77.6 reduce-scatter.4
